TPU v7x, 256 devices: a whole 4x4x8 slice. The times are simulated.
256 devices in a mesh: dp: 4 (over x), space: 64 (over y, z, core).
Axes of the slice: x: 4, y: 4, z: 8, core: 2. Of those that a mesh axis runs over, the one named last changes fastest.
Arguments:
- features: bfloat16 [4, 64, 96, 1024], P('dp', 'space'), may hold values from -6 to 6
- cotangent: bfloat16 [4, 64, 192, 128], P('dp', 'space'), may hold values from -6 to 6
- conv_weight: bfloat16 [96, 2592], replicated, may hold values from -0.125 to 0.125
- down_weight: bfloat16 [192, 768], replicated, may hold values from -0.21875 to 0.21875
- neighbours: int32 [4, 64, 26], P('dp', 'space'), may hold values from -1 to 63, as said below
Outputs:
- coarse_out: bfloat16 [4, 64, 192, 128], P('dp', 'space')
- grad_features: float32 [4, 64, 96, 1024], P('dp', 'space')
- grad_conv: float32 [96, 2592], replicated
- grad_down: float32 [192, 768], replicated
Inputs may be any that keep to these rules, and one draw needn't show every extreme that they name: The blocks of a tile sit at distinct cells of a grid; if neighbours[t, s, d] = p is not -1 then neighbours[t, p, 25 - d] = s; a row never names its own block and names a device at most once.
All inputs are finite; a program needn't handle non-finite values.
Results may differ from a plain program's by a relative error of at most 0.0095.
Values may be sent and summed in bfloat16 or wider, within the bound.
No kernel may reach another device: no remote copies, remote signals or barrier semaphores. Data moves between devices by JAX's collectives and lax.ppermute only.
A program may use at most 128 MiB of HBM per device.

v0:
```python
import jax
import jax.numpy as jnp
from jax import lax
from jax.sharding import PartitionSpec as P

BRICK = 8
DIRECTIONS = [
    (step_x, step_y, step_z)
    for step_x in (-1, 0, 1)
    for step_y in (-1, 0, 1)
    for step_z in (-1, 0, 1)
    if (step_x, step_y, step_z) != (0, 0, 0)
]
EPSILON = 1e-06


def cut_inner(offset, extent):
    if offset < 0:
        return slice(0, 1)
    if offset > 0:
        return slice(extent - 1, extent)
    return slice(0, extent)


def cut_outer(offset, extent):
    if offset < 0:
        return slice(0, 1)
    if offset > 0:
        return slice(extent + 1, extent + 2)
    return slice(1, extent + 1)


def inner_layer(block_data, offset):
    return block_data[
        :,
        cut_inner(offset[0], block_data.shape[1]),
        cut_inner(offset[1], block_data.shape[2]),
        cut_inner(offset[2], block_data.shape[3]),
    ]


def outer_layer(padded, offset):
    return padded[
        :,
        cut_outer(offset[0], padded.shape[1] - 2),
        cut_outer(offset[1], padded.shape[2] - 2),
        cut_outer(offset[2], padded.shape[3] - 2),
    ]


def conv_taps(padded, weight_matrix):
    channels = padded.shape[0]
    size_x, size_y, size_z = (padded.shape[1] - 2, padded.shape[2] - 2, padded.shape[3] - 2)
    accumulated = jnp.zeros((weight_matrix.shape[0], size_x * size_y * size_z), jnp.float32)
    for step_x in range(3):
        for step_y in range(3):
            columns = jnp.concatenate(
                [
                    padded[
                        :,
                        step_x : step_x + size_x,
                        step_y : step_y + size_y,
                        step_z : step_z + size_z,
                    ]
                    for step_z in range(3)
                ],
                axis=0,
            ).reshape(3 * channels, size_x * size_y * size_z)
            start_col = (step_x * 3 + step_y) * 3 * channels
            accumulated = accumulated + jnp.dot(
                weight_matrix[:, start_col : start_col + 3 * channels],
                columns,
                preferred_element_type=jnp.float32,
            )
    return accumulated


def weight_taps(padded, grad_out):
    channels = padded.shape[0]
    size_x, size_y, size_z = (padded.shape[1] - 2, padded.shape[2] - 2, padded.shape[3] - 2)
    blocks_out = []
    for step_x in range(3):
        for step_y in range(3):
            columns = jnp.concatenate(
                [
                    padded[
                        :,
                        step_x : step_x + size_x,
                        step_y : step_y + size_y,
                        step_z : step_z + size_z,
                    ]
                    for step_z in range(3)
                ],
                axis=0,
            ).reshape(3 * channels, size_x * size_y * size_z)
            blocks_out.append(
                lax.dot_general(
                    grad_out, columns, (((1,), (1,)), ((), ())), preferred_element_type=jnp.float32
                )
            )
    return jnp.concatenate(blocks_out, axis=1)


def flipped(weight_matrix):
    channels = weight_matrix.shape[0]
    return (
        weight_matrix.reshape(channels, 27, channels)[:, ::-1, :]
        .transpose(2, 1, 0)
        .reshape(channels, 27 * channels)
    )


def coarse_patches(hidden_block):
    channels, size_x, size_y, size_z = hidden_block.shape
    split = hidden_block.reshape(channels, size_x // 2, 2, size_y // 2, 2, size_z // 2, 2)
    return split.transpose(2, 4, 6, 0, 1, 3, 5).reshape(
        8 * channels, size_x // 2 * (size_y // 2) * (size_z // 2)
    )


def from_patches(patch_data, channels, size_x, size_y, size_z):
    split = patch_data.reshape(2, 2, 2, channels, size_x // 2, size_y // 2, size_z // 2)
    return split.transpose(3, 4, 0, 5, 1, 6, 2).reshape(channels, size_x * size_y * size_z)


def silu_slope(activation):
    sigmoid_value = jax.nn.sigmoid(activation)
    return sigmoid_value * (1.0 + activation * (1.0 - sigmoid_value))


def normalized(accumulated):
    return accumulated * lax.rsqrt(jnp.mean(accumulated * accumulated) + EPSILON)


def shards(features, cotangent, conv_weight, down_weight, neighbours):
    channels = features.shape[2]
    block_side = BRICK
    block_depth = features.shape[3] // (block_side * block_side)
    peer_count = lax.axis_size("space")
    capacity = max(block_side * block_side, block_side * block_depth)
    owner_row = neighbours[0, 0]
    present = owner_row >= 0
    target = jnp.where(present, owner_row, peer_count)
    source = jnp.clip(owner_row, 0, peer_count - 1)

    def pack_faces(face_layers, wire_type):
        stacked = jnp.stack(
            [
                jnp.pad(
                    face_layer.reshape(channels, -1), ((0, 0), (0, capacity - face_layer[0].size))
                )
                for face_layer in face_layers
            ]
        )
        return (
            jnp.zeros((peer_count, channels, capacity), wire_type)
            .at[target]
            .set(stacked, mode="drop")
        )

    def unpack_faces(received, shapes):
        picked = jnp.take(received, source, axis=0) * present[:, None, None].astype(received.dtype)
        pieces = []
        for number, shape in enumerate(shapes):
            count = shape[1] * shape[2] * shape[3]
            pieces.append(picked[number, :, :count].reshape(shape))
        return pieces

    def fill_rim(block_data, received):
        padded = jnp.pad(block_data, ((0, 0), (1, 1), (1, 1), (1, 1)))
        pieces = unpack_faces(
            received, [inner_layer(block_data, offset).shape for offset in DIRECTIONS]
        )
        for offset, face_piece in zip(DIRECTIONS, pieces):
            padded = padded.at[
                :,
                cut_outer(offset[0], block_side),
                cut_outer(offset[1], block_side),
                cut_outer(offset[2], block_depth),
            ].set(face_piece)
        return padded

    own_block = features[0, 0].reshape(channels, block_side, block_side, block_depth)
    sent = pack_faces([inner_layer(own_block, offset) for offset in DIRECTIONS], jnp.bfloat16)
    received = lax.all_to_all(sent, "space", split_axis=0, concat_axis=0, tiled=True)
    padded = fill_rim(own_block, received)
    preact = conv_taps(padded, conv_weight)
    hidden = jax.nn.silu(preact).astype(jnp.bfloat16)
    patches = coarse_patches(hidden.reshape(channels, block_side, block_side, block_depth))
    coarse_out = jnp.dot(down_weight, patches, preferred_element_type=jnp.float32).astype(
        jnp.bfloat16
    )
    cot_block = cotangent[0, 0]
    down_part = lax.dot_general(
        cot_block, patches, (((1,), (1,)), ((), ())), preferred_element_type=jnp.float32
    )
    spread_back = from_patches(
        jnp.dot(down_weight.T, cot_block, preferred_element_type=jnp.float32),
        channels,
        block_side,
        block_side,
        block_depth,
    )
    grad_pre = (spread_back * silu_slope(preact)).astype(jnp.bfloat16)
    conv_part = weight_taps(padded, grad_pre)
    flip_weight = flipped(conv_weight)
    grad_block = grad_pre.reshape(channels, block_side, block_side, block_depth)
    widened = jnp.pad(grad_block, ((0, 0), (2, 2), (2, 2), (2, 2)))
    full_grad = conv_taps(widened, flip_weight).reshape(
        channels, block_side + 2, block_side + 2, block_depth + 2
    )
    spill_buffer = pack_faces(
        [outer_layer(full_grad, offset) for offset in DIRECTIONS], jnp.float32
    )
    got_spill = lax.all_to_all(
        spill_buffer.astype(jnp.bfloat16), "space", split_axis=0, concat_axis=0, tiled=True
    ).astype(spill_buffer.dtype)
    inner_part = full_grad[:, 1:-1, 1:-1, 1:-1]
    pieces = unpack_faces(
        got_spill, [inner_layer(inner_part, offset).shape for offset in DIRECTIONS]
    )
    for offset, face_piece in zip(DIRECTIONS, pieces):
        inner_part = inner_part.at[
            :,
            cut_inner(offset[0], block_side),
            cut_inner(offset[1], block_side),
            cut_inner(offset[2], block_depth),
        ].add(face_piece)
    grad_features = inner_part.reshape(channels, -1)
    conv_sum, down_sum = lax.psum((conv_part, down_part), ("dp", "space"))
    return (
        coarse_out[None, None],
        grad_features[None, None],
        normalized(conv_sum),
        normalized(down_sum),
    )


def solution(mesh):
    placed = (
        P("dp", "space", None, None),
        P("dp", "space", None, None),
        P(),
        P(),
        P("dp", "space", None),
    )
    return jax.shard_map(
        shards,
        mesh=mesh,
        in_specs=placed,
        out_specs=(P("dp", "space", None, None), P("dp", "space", None, None), P(), P()),
        check_vma=False,
    )
```

profile of v0, /device:TPU:2, one launch (start us, length us, event | category | flops | bytes accessed | tf_op | source)
XLA Modules:
  0.0 610.5 jit_solution(4286179501511224729)
XLA Ops:
  10.8 5.3 scatter_fusion
  16.1 12.1 %all-to-all-start = ((bf16[64,96,128]{2,1,0:T(8,128)(2,1)}), bf16[64,96,128]{2,1,0:T(8,128)(2,1)S(1)}, u32[]{:S(2)}, u32[]{:S(2)}) async-start(bf16[64,96,128]{2,1,0:T(8,128)(2,1)} %scatter_fusion), calls=%async_computation | async-start | bytes 3145728 | tf_op jit(solution)/shard_map/all_to_all | solution.py:185
  31.8 35.9 %all-to-all-done = bf16[64,96,128]{2,1,0:T(8,128)(2,1)S(1)} async-done(((bf16[64,96,128]{2,1,0:T(8,128)(2,1)}), bf16[64,96,128]{2,1,0:T(8,128)(2,1)S(1)}, u32[]{:S(2)}, u32[]{:S(2)}) %all-to-all-start) | async-done | bytes 1572896 | tf_op jit(solution)/shard_map/all_to_all | solution.py:185
  89.4 2.0 multiply_convert_fusion
  96.3 5.5 pad_slice_fusion.2
  101.9 2.2 pad_slice_fusion.1
  105.8 2.4 pad_maximum_fusion.7
  108.2 1.9 reshape.2479
  110.1 2.4 pad_maximum_fusion.6
  112.5 1.9 reshape.2478
  114.4 2.4 pad_maximum_fusion.5
  116.8 1.9 reshape.2477
  118.7 2.4 pad_maximum_fusion.4
  121.1 1.9 reshape.2476
  123.0 2.4 pad_maximum_fusion.3
  125.4 1.9 reshape.2475
  127.2 2.6 pad_maximum_fusion.2
  129.8 1.9 reshape.2474
  131.7 2.4 pad_maximum_fusion.1
  134.1 1.9 reshape.2473
  135.9 2.4 pad_maximum_fusion
  138.3 1.9 reshape.2470
  140.2 2.1 fusion.13
  153.0 1.6 copy.157
  154.9 3.7 scatter_fusion.1
  160.1 7.0 %all-to-all-start.1 = ((bf16[64,96,128]{2,1,0:T(8,128)(2,1)}), bf16[64,96,128]{2,1,0:T(8,128)(2,1)}, u32[]{:S(2)}, u32[]{:S(2)}) async-start(bf16[64,96,128]{2,1,0:T(8,128)(2,1)} %convert_element_type.100), calls=%async_computation.1 | async-start | bytes 3145728 | tf_op jit(solution)/shard_map/all_to_all | solution.py:215
  175.2 2.0 and_reduce_fusion
  177.2 2.0 slice.2776
  179.3 1.9 copy.225
  181.2 1.8 fusion.2
  183.0 257.4 %all-reduce.49.cloned.1.call-done = (f32[96,2592]{1,0:T(8,128)}, f32[192,768]{1,0:T(8,128)}) async-done(((f32[96,2592]{1,0:T(8,128)}, f32[192,768]{1,0:T(8,128)}), (f32[96,2592]{1,0:T(8,128)}, f32[192,768]{1,0:T(8,128)})) %all-reduce.49.cloned.1.call-update) | async-done | bytes 1585168 | tf_op jit(solution)/shard_map/psum | solution.py:230
  440.5 1.8 multiply_reduce_fusion.1
  443.0 2.1 multiply_reduce_fusion
  445.8 2.0 broadcast_multiply_fusion.1
  448.8 3.5 convert_element_type.101
  452.3 3.6 gather_fusion.1
  455.9 1.5 select_multiply_fusion
  459.5 1.5 fusion.34
  461.0 1.7 slice_bitcast_fusion.3
  462.7 1.6 fusion.46
  469.1 2.6 scatter-add.91
  476.0 2.8 add_select_fusion.1
  478.8 4.6 scatter-add.95
  484.4 2.6 fusion.25
  488.5 2.2 copy.169
  491.7 3.0 scatter-add.101
  499.0 2.8 add_select_fusion
  501.8 4.8 scatter-add.105
  507.5 2.3 copy.175
  509.7 4.2 slice_add_fusion.1
  513.9 18.6 %scatter-add.106 = f32[96,8,8,16]{3,0,2,1:T(8,128)S(1)} dynamic-update-slice(f32[96,8,8,16]{3,0,2,1:T(8,128)S(1)} %scatter-add.105, f32[96,8,8,1]{3,0,2,1:T(8,128)} %slice_add_fusion.1, s32[]{:T(128)} %constant.1634.clone.1, s32[]{:T(128)} %constant.1634.clone.1, s32[]{:T(128)} %constant.1634.clone.1, s32[]{:T(128)} %constant.1634.clone.1) | dynamic-update-slice | bytes 49156 | tf_op jit(solution)/shard_map/scatter-add | solution.py:228
  532.6 2.2 copy.177
  534.9 4.4 slice_add_fusion
  539.3 23.3 %scatter-add.109 = f32[96,8,8,16]{3,0,2,1:T(8,128)S(1)} dynamic-update-slice(f32[96,8,8,16]{3,0,2,1:T(8,128)S(1)} %scatter-add.106, f32[96,8,8,1]{3,0,2,1:T(8,128)} %slice_add_fusion, s32[]{:T(128)} %constant.1634.clone.1, s32[]{:T(128)} %constant.1634.clone.1, s32[]{:T(128)} %constant.1634.clone.1, s32[]{:T(128)} %constant.1644.clone.1) | dynamic-update-slice | bytes 49156 | tf_op jit(solution)/shard_map/scatter-add | solution.py:228
  565.0 3.0 scatter-add.110
  568.0 1.5 copy.180
  570.5 2.2 copy.183
  573.9 3.6 scatter-add.114
  584.5 2.6 scatter-add.120
  587.1 1.5 copy.188
  589.6 2.2 copy.191
  592.9 3.3 scatter-add.124
  599.3 1.8 copy.194
  601.1 2.0 copy.195
  (323 shorter events, 92.7 us)
Async XLA Ops:
  8.3 1.1 copy-start.39
  16.1 12.3 %copy-start.22 = (bf16[192,768]{1,0:T(8,128)(2,1)S(1)}, bf16[192,768]{1,0:T(8,128)(2,1)}, u32[]{:S(2)}) copy-start(bf16[192,768]{1,0:T(8,128)(2,1)} %param.112) | copy-start | bytes 884740
  16.1 12.5 %copy-start.32 = (bf16[1,1,192,128]{3,2,1,0:T(8,128)(2,1)S(1)}, bf16[1,1,192,128]{3,2,1,0:T(8,128)(2,1)}, u32[]{:S(2)}) copy-start(bf16[1,1,192,128]{3,2,1,0:T(8,128)(2,1)} %param.110) | copy-start | bytes 147460
  16.1 51.6 %all-to-all-start = ((bf16[64,96,128]{2,1,0:T(8,128)(2,1)}), bf16[64,96,128]{2,1,0:T(8,128)(2,1)S(1)}, u32[]{:S(2)}, u32[]{:S(2)}) async-start(bf16[64,96,128]{2,1,0:T(8,128)(2,1)} %scatter_fusion), calls=%async_computation | async-start | bytes 3145728 | tf_op jit(solution)/shard_map/all_to_all | solution.py:185
  28.6 1.8 copy-start.19
  75.3 3.2 copy-start
  77.1 3.2 copy-start.2
  78.9 3.2 copy-start.4
  80.7 3.1 copy-start.6
  87.6 1.8 copy-start.30
  140.2 2.1 copy-start.14
  140.2 2.1 copy-start.18
  142.3 1.3 copy-start.13
  143.6 1.3 copy-start.12
  145.0 1.3 copy-start.11
  146.3 1.3 copy-start.10
  147.7 1.3 copy-start.9
  149.0 1.3 copy-start.8
  151.9 1.1 copy-start.17
  160.1 7.1 %copy-start.7 = (bf16[288,8,8,16]{0,3,2,1:T(8,128)(2,1)S(1)}, bf16[288,8,8,16]{0,3,2,1:T(8,128)(2,1)}, u32[]{:S(2)}) copy-start(bf16[288,8,8,16]{0,3,2,1:T(8,128)(2,1)} %copy-done.6) | copy-start | bytes 1769476
  160.1 8.0 %copy-start.31 = (bf16[96,1024]{1,0:T(8,128)(2,1)S(1)}, bf16[96,1024]{1,0:T(8,128)(2,1)}, u32[]{:S(2)}) copy-start(bf16[96,1024]{1,0:T(8,128)(2,1)} %get-tuple-element.737) | copy-start | bytes 589828
  160.1 288.7 %all-to-all-start.1 = ((bf16[64,96,128]{2,1,0:T(8,128)(2,1)}), bf16[64,96,128]{2,1,0:T(8,128)(2,1)}, u32[]{:S(2)}, u32[]{:S(2)}) async-start(bf16[64,96,128]{2,1,0:T(8,128)(2,1)} %convert_element_type.100), calls=%async_computation.1 | async-start | bytes 3145728 | tf_op jit(solution)/shard_map/all_to_all | solution.py:215
  167.1 1.7 copy-start.5
  167.1 2.7 copy-start.3
  167.1 273.4 %all-reduce.49.cloned.1.call-start = ((), (), s32[]{:S(2)}) async-start(), calls=%async_computation.2 | async-start | bytes 3244032 | tf_op jit(solution)/shard_map/psum | solution.py:230
  168.3 1.8 copy-start.1
  168.8 1.6 copy-start.23
  168.8 1.6 copy-start.24
  168.8 1.6 copy-start.25
  168.8 1.6 copy-start.26
  168.8 1.6 copy-start.27
  169.8 0.9 copy-start.28
  169.8 1.0 copy-start.29
  170.1 2.0 copy-start.33
  172.1 2.3 copy-start.36
  172.1 3.1 copy-start.37
  172.1 3.1 copy-start.38
  445.8 2.0 copy-start.16
  457.4 1.1 copy-start.15
  513.9 18.6 %copy-start.35 = (f32[1,96,64]{2,1,0:T(8,128)S(1)}, f32[1,96,64]{2,1,0:T(8,128)}, u32[]{:S(2)}) copy-start(f32[1,96,64]{2,1,0:T(8,128)} %get-tuple-element.662) | copy-start | bytes 73732
  539.3 23.3 %copy-start.34 = (f32[96,8,1,1]{1,0,3,2:T(8,128)S(1)}, f32[96,8,1,1]{1,0,3,2:T(8,128)}, u32[]{:S(2)}) copy-start(f32[96,8,1,1]{1,0,3,2:T(8,128)} %get-tuple-element.653) | copy-start | bytes 9220
  572.7 1.0 copy-start.20
  591.8 1.0 copy-start.21
Sparse Core Ops, SparseCore 0:
  174.0 266.4 all-reduce.48
where the time goes:
time: 620 us; the launch traced here: 610 us
  waiting for transfers between devices  293 us (47%)
  local copies, waits for them, and re-layouts  177 us (29%)
  other arithmetic  73.2 us (12%)
  matrix products  29.7 us (5%)
  starting transfers between devices  19.2 us (3%)
  between operations  17.5 us (3%)
    psum x1, waiting for transfers between devices, shards(): conv_sum, down_sum = lax.psum((conv_part, down_part), ('dp', 'space'))  257 us
    scatter-add x22, local copies, waits for them, and re-layouts, shards(): inner_part = inner_part.at[:, cut_inner(offset[0], block_side), cut_inner...  75.3 us
    all_to_all x1, waiting for transfers between devices, shards(): lax.all_to_all(sent, 'space', split_axis=0, concat_axis=0, tiled=True)  35.9 us
    another operation x33, local copies, waits for them, and re-layouts  26 us
    concatenate x18, other arithmetic, conv_taps(): jnp.concatenate([padded[:, step_x:step_x + size_x, step_y:step_y + size_y...  24 us
    add x19, other arithmetic, shards(): inner_part = inner_part.at[:, cut_inner(offset[0], block_side), cut_inner...  22.2 us
    dot_general x18, matrix products, conv_taps(): jnp.dot(weight_matrix[:, start_col:start_col + 3 * channels], columns, pr...  19.3 us
    reshape x9, local copies, waits for them, and re-layouts, conv_taps(): columns = jnp.concatenate([padded[:, step_x:step_x + size_x, step_y:step_...  15.8 us
  transfers between devices with their start and end apart: 3, of which 2 were waited for; matrix products, arithmetic and copies ran while one was open for 4% of the time, Pallas kernels for 0%

commit v1 on v0

--- a/solution.py
+++ b/solution.py
@@ -12,6 +12,14 @@
     if (step_x, step_y, step_z) != (0, 0, 0)
 ]
 EPSILON = 1e-06
+
+
+def mark_group_here(state):
+    ax_name = "dp"
+    mesh_name = "space"
+    for ii in (mesh_name, ax_name):
+        state = lax.psum(state, axis_name=ii)
+    return state
 
 
 def cut_inner(offset, extent):
@@ -227,7 +235,7 @@
             cut_inner(offset[2], block_depth),
         ].add(face_piece)
     grad_features = inner_part.reshape(channels, -1)
-    conv_sum, down_sum = lax.psum((conv_part, down_part), ("dp", "space"))
+    conv_sum, down_sum = mark_group_here((conv_part, down_part))
     return (
         coarse_out[None, None],
         grad_features[None, None],

time: 620 us -> 598 us (0.965)
  waiting for transfers between devices: 293 us -> 262 us
  local copies, waits for them, and re-layouts: 177 us -> 184 us
    psum x1 -> x2, waiting for transfers between devices: 257 us -> 226 us  [mark_group_here(): state = lax.psum(state, axis_name=ii)]
    unnamed x141 -> x171, local copies, waits for them, and re-layouts: 14.3 us -> 15.2 us
  transfers between devices with their start and end apart: 3 -> 4, of which waited for: 2 -> 3; matrix products, arithmetic and copies ran while one was open for 4% -> 5% of each run, Pallas kernels for 0% -> 0%
where the time goes in v1:
time: 598 us; the launch traced here: 587 us
  waiting for transfers between devices  262 us (44%)
  local copies, waits for them, and re-layouts  184 us (31%)
  other arithmetic  74.2 us (12%)
  matrix products  30 us (5%)
  starting transfers between devices  19 us (3%)
  between operations  17.6 us (3%)
    psum x2, waiting for transfers between devices, mark_group_here(): state = lax.psum(state, axis_name=ii)  226 us
    scatter-add x22, local copies, waits for them, and re-layouts, shards(): inner_part = inner_part.at[:, cut_inner(offset[0], block_side), cut_inner...  75.3 us
    all_to_all x1, waiting for transfers between devices, shards(): lax.all_to_all(sent, 'space', split_axis=0, concat_axis=0, tiled=True)  35.3 us
    another operation x33, local copies, waits for them, and re-layouts  26.1 us
    concatenate x18, other arithmetic, conv_taps(): jnp.concatenate([padded[:, step_x:step_x + size_x, step_y:step_y + size_y...  24 us
    add x19, other arithmetic, shards(): inner_part = inner_part.at[:, cut_inner(offset[0], block_side), cut_inner...  22.2 us
    dot_general x18, matrix products, conv_taps(): jnp.dot(weight_matrix[:, start_col:start_col + 3 * channels], columns, pr...  18.9 us
    reshape x9, local copies, waits for them, and re-layouts, conv_taps(): columns = jnp.concatenate([padded[:, step_x:step_x + size_x, step_y:step_...  15.9 us
  transfers between devices with their start and end apart: 4, of which 3 were waited for; matrix products, arithmetic and copies ran while one was open for 5% of the time, Pallas kernels for 0%

profile of v1, /device:TPU:2, one launch (start us, length us, event | category | flops | bytes accessed | tf_op | source)
XLA Modules:
  0.0 586.6 jit_solution(12996974185497361109)
XLA Ops:
  10.8 5.3 scatter_fusion
  16.1 12.1 %all-to-all-start = ((bf16[64,96,128]{2,1,0:T(8,128)(2,1)}), bf16[64,96,128]{2,1,0:T(8,128)(2,1)S(1)}, u32[]{:S(2)}, u32[]{:S(2)}) async-start(bf16[64,96,128]{2,1,0:T(8,128)(2,1)} %scatter_fusion), calls=%async_computation | async-start | bytes 3145728 | tf_op jit(solution)/shard_map/all_to_all | solution.py:193
  32.4 35.3 %all-to-all-done = bf16[64,96,128]{2,1,0:T(8,128)(2,1)S(1)} async-done(((bf16[64,96,128]{2,1,0:T(8,128)(2,1)}), bf16[64,96,128]{2,1,0:T(8,128)(2,1)S(1)}, u32[]{:S(2)}, u32[]{:S(2)}) %all-to-all-start) | async-done | bytes 1572896 | tf_op jit(solution)/shard_map/all_to_all | solution.py:193
  88.9 2.0 multiply_convert_fusion
  99.0 5.5 pad_slice_fusion.2
  104.6 2.2 pad_slice_fusion.1
  108.5 2.4 pad_maximum_fusion.7
  110.9 1.9 reshape.2479
  112.8 2.4 pad_maximum_fusion.6
  115.2 1.9 reshape.2478
  117.1 2.4 pad_maximum_fusion.5
  119.5 1.9 reshape.2477
  121.4 2.4 pad_maximum_fusion.4
  123.8 1.9 reshape.2476
  125.7 2.4 pad_maximum_fusion.3
  128.1 1.9 reshape.2475
  130.0 2.6 pad_maximum_fusion.2
  132.6 1.9 reshape.2474
  134.4 2.4 pad_maximum_fusion.1
  136.8 1.9 reshape.2473
  138.7 2.4 pad_maximum_fusion
  141.1 1.9 reshape.2470
  143.0 2.1 fusion.13
  161.5 2.3 concatenate.266
  165.3 1.5 copy.157
  167.5 3.9 scatter_fusion.1
  172.8 6.8 %all-to-all-start.1 = ((bf16[64,96,128]{2,1,0:T(8,128)(2,1)}), bf16[64,96,128]{2,1,0:T(8,128)(2,1)}, u32[]{:S(2)}, u32[]{:S(2)}) async-start(bf16[64,96,128]{2,1,0:T(8,128)(2,1)} %convert_element_type.100), calls=%async_computation.1 | async-start | bytes 3145728 | tf_op jit(solution)/shard_map/all_to_all | solution.py:223
  179.7 182.0 %all-reduce.51.cloned.1.call-done = (f32[96,2592]{1,0:T(8,128)}, f32[192,768]{1,0:T(8,128)}) async-done(((f32[96,2592]{1,0:T(8,128)}, f32[192,768]{1,0:T(8,128)}), (f32[96,2592]{1,0:T(8,128)}, f32[192,768]{1,0:T(8,128)})) %all-reduce.51.cloned.1.call-update) | async-done | bytes 1585168 | tf_op jit(solution)/shard_map/psum | solution.py:21
  363.8 2.1 and_reduce_fusion
  365.9 2.0 slice.2776
  368.0 1.9 copy.225
  369.9 1.8 fusion.2
  371.7 44.4 %all-reduce.53.cloned.1.call-done = (f32[96,2592]{1,0:T(8,128)}, f32[192,768]{1,0:T(8,128)}) async-done(((f32[96,2592]{1,0:T(8,128)}, f32[192,768]{1,0:T(8,128)}), (f32[96,2592]{1,0:T(8,128)}, f32[192,768]{1,0:T(8,128)})) %all-reduce.53.cloned.1.call-update) | async-done | bytes 1585168 | tf_op jit(solution)/shard_map/psum | solution.py:21
  416.1 1.8 multiply_reduce_fusion.1
  418.6 2.1 multiply_reduce_fusion
  421.4 2.0 broadcast_multiply_fusion.1
  424.5 3.5 convert_element_type.101
  428.0 3.7 gather_fusion.1
  436.9 1.7 slice_bitcast_fusion.3
  438.6 1.5 fusion.46
  445.0 2.6 scatter-add.91
  451.9 2.9 add_select_fusion.1
  454.8 4.7 scatter-add.95
  460.5 2.8 fusion.25
  464.5 2.2 copy.169
  467.7 3.2 scatter-add.101
  475.3 2.9 add_select_fusion
  478.1 4.9 scatter-add.105
  483.9 2.2 copy.175
  486.2 4.2 slice_add_fusion.1
  490.3 18.6 %scatter-add.106 = f32[96,8,8,16]{3,0,2,1:T(8,128)S(1)} dynamic-update-slice(f32[96,8,8,16]{3,0,2,1:T(8,128)S(1)} %scatter-add.105, f32[96,8,8,1]{3,0,2,1:T(8,128)} %slice_add_fusion.1, s32[]{:T(128)} %constant.1634.clone.1, s32[]{:T(128)} %constant.1634.clone.1, s32[]{:T(128)} %constant.1634.clone.1, s32[]{:T(128)} %constant.1634.clone.1) | dynamic-update-slice | bytes 49156 | tf_op jit(solution)/shard_map/scatter-add | solution.py:236
  509.0 2.3 copy.177
  511.3 4.5 slice_add_fusion
  515.8 23.3 %scatter-add.109 = f32[96,8,8,16]{3,0,2,1:T(8,128)S(1)} dynamic-update-slice(f32[96,8,8,16]{3,0,2,1:T(8,128)S(1)} %scatter-add.106, f32[96,8,8,1]{3,0,2,1:T(8,128)} %slice_add_fusion, s32[]{:T(128)} %constant.1634.clone.1, s32[]{:T(128)} %constant.1634.clone.1, s32[]{:T(128)} %constant.1634.clone.1, s32[]{:T(128)} %constant.1644.clone.1) | dynamic-update-slice | bytes 49156 | tf_op jit(solution)/shard_map/scatter-add | solution.py:236
  541.5 3.0 scatter-add.110
  544.5 1.5 copy.180
  547.0 2.2 copy.183
  550.4 3.6 scatter-add.114
  560.7 2.6 scatter-add.120
  563.2 1.5 copy.188
  565.8 2.2 copy.191
  569.1 3.3 scatter-add.124
  575.5 1.8 copy.194
  577.3 2.0 copy.195
  (356 shorter events, 100.0 us)
Async XLA Ops:
  8.3 1.1 copy-start.54
  9.4 6.7 %copy-start.40 = (s32[26]{0:T(128)}, s32[26]{0:T(128)S(1)}, u32[]{:S(2)}) copy-start(s32[26]{0:T(128)S(1)} %get-tuple-element.800) | copy-start | bytes 316
  16.1 12.3 %copy-start.14 = (bf16[192,768]{1,0:T(8,128)(2,1)S(1)}, bf16[192,768]{1,0:T(8,128)(2,1)}, u32[]{:S(2)}) copy-start(bf16[192,768]{1,0:T(8,128)(2,1)} %param.112) | copy-start | bytes 884740
  16.1 12.5 %copy-start.20 = (bf16[1,1,192,128]{3,2,1,0:T(8,128)(2,1)S(1)}, bf16[1,1,192,128]{3,2,1,0:T(8,128)(2,1)}, u32[]{:S(2)}) copy-start(bf16[1,1,192,128]{3,2,1,0:T(8,128)(2,1)} %param.110) | copy-start | bytes 147460
  16.1 51.6 %all-to-all-start = ((bf16[64,96,128]{2,1,0:T(8,128)(2,1)}), bf16[64,96,128]{2,1,0:T(8,128)(2,1)S(1)}, u32[]{:S(2)}, u32[]{:S(2)}) async-start(bf16[64,96,128]{2,1,0:T(8,128)(2,1)} %scatter_fusion), calls=%async_computation | async-start | bytes 3145728 | tf_op jit(solution)/shard_map/all_to_all | solution.py:193
  28.2 333.5 %all-reduce.51.cloned.1.call-start = ((), (), s32[]{:S(2)}) async-start(), calls=%async_computation.2 | async-start | bytes 3244032 | tf_op jit(solution)/shard_map/psum | solution.py:21
  28.6 1.8 copy-start.11
  31.8 36.9 %copy-start.37 = (s32[1024]{0:T(1024)}, s32[1024]{0:T(1024)S(1)}, u32[]{:S(2)}) copy-start(s32[1024]{0:T(1024)S(1)} %pad_clamp_fusion) | copy-start | bytes 12292
  31.9 36.9 %copy-start.38 = (pred[26]{0:T(512)(128)(4,1)}, pred[26]{0:T(512)(128)(4,1)S(1)}, u32[]{:S(2)}) copy-start(pred[26]{0:T(512)(128)(4,1)S(1)} %compare_and_fusion) | copy-start | bytes 82
  87.1 1.8 copy-start.16
  143.0 2.1 copy-start.6
  143.0 2.1 copy-start.10
  145.1 1.3 copy-start.5
  146.4 1.3 copy-start.4
  147.8 1.3 copy-start.3
  149.1 1.3 copy-start.2
  150.5 1.3 copy-start.1
  151.8 1.3 copy-start
  154.6 4.5 copy-start.19
  154.6 5.2 copy-start.21
  154.7 9.1 %copy-start.9 = (f32[96,10,10,18]{0,3,2,1:T(8,128)}, f32[96,10,10,18]{0,3,2,1:T(8,128)S(1)}, u32[]{:S(2)}) copy-start(f32[96,10,10,18]{0,3,2,1:T(8,128)S(1)} %reshape.2481) | copy-start | bytes 2073604
  154.7 6.8 %copy-start.15 = (f32[96,288]{1,0:T(8,128)S(1)}, f32[96,288]{1,0:T(8,128)}, u32[]{:S(2)}) copy-start(f32[96,288]{1,0:T(8,128)} %fusion.71) | copy-start | bytes 331780
  163.8 0.9 copy-start.49
  163.8 1.0 copy-start.36
  163.8 1.0 copy-start.18
  163.8 1.0 copy-start.35
  163.8 1.0 copy-start.48
  163.8 1.0 copy-start.28
  163.8 1.0 copy-start.47
  163.8 1.0 copy-start.34
  163.8 1.1 copy-start.17
  163.9 1.1 copy-start.33
  163.9 1.1 copy-start.25
  163.9 1.1 copy-start.24
  163.9 1.1 copy-start.32
  163.9 1.1 copy-start.31
  163.9 1.2 copy-start.46
  163.9 1.2 copy-start.27
  163.9 1.2 copy-start.45
  163.9 1.2 copy-start.30
  163.9 1.2 copy-start.29
  164.0 1.2 copy-start.44
  164.0 1.3 copy-start.26
  164.0 1.3 copy-start.43
  166.8 0.7 copy-start.41
  172.8 190.2 %copy-start.51 = (s32[4]{0:T(128)S(1)}, s32[4]{0:T(128)}, u32[]{:S(2)}) copy-start(s32[4]{0:T(128)} %constant.1649.clone.1) | copy-start | bytes 52
  172.8 191.0 %copy-start.52 = (s32[4]{0:T(128)S(1)}, s32[4]{0:T(128)}, u32[]{:S(2)}) copy-start(s32[4]{0:T(128)} %constant.1646.clone.1) | copy-start | bytes 52
  172.8 191.0 %copy-start.53 = (s32[4]{0:T(128)S(1)}, s32[4]{0:T(128)}, u32[]{:S(2)}) copy-start(s32[4]{0:T(128)} %constant.1650.clone.1) | copy-start | bytes 52
  172.8 251.6 %all-to-all-start.1 = ((bf16[64,96,128]{2,1,0:T(8,128)(2,1)}), bf16[64,96,128]{2,1,0:T(8,128)(2,1)}, u32[]{:S(2)}, u32[]{:S(2)}) async-start(bf16[64,96,128]{2,1,0:T(8,128)(2,1)} %convert_element_type.100), calls=%async_computation.1 | async-start | bytes 3145728 | tf_op jit(solution)/shard_map/all_to_all | solution.py:223
  179.6 188.2 %copy-start.42 = (f32[96,1,1,1]{0,3,2,1:T(1,128)S(1)}, f32[96,1,1,1]{0,3,2,1:T(1,128)}, u32[]{:S(2)}) copy-start(f32[96,1,1,1]{0,3,2,1:T(1,128)} %get-tuple-element.667) | copy-start | bytes 1156
  179.6 236.5 %all-reduce.53.cloned.1.call-start = ((), (), s32[]{:S(2)}) async-start(), calls=%async_computation.3 | async-start | bytes 3244032 | tf_op jit(solution)/shard_map/psum | solution.py:21
  421.4 2.0 copy-start.8
  428.0 3.7 copy-start.39
  428.0 3.7 copy-start.50
  433.3 1.1 copy-start.7
  490.3 18.6 %copy-start.23 = (f32[1,96,64]{2,1,0:T(8,128)S(1)}, f32[1,96,64]{2,1,0:T(8,128)}, u32[]{:S(2)}) copy-start(f32[1,96,64]{2,1,0:T(8,128)} %get-tuple-element.664) | copy-start | bytes 73732
  515.8 23.3 %copy-start.22 = (f32[96,8,1,1]{1,0,3,2:T(8,128)S(1)}, f32[96,8,1,1]{1,0,3,2:T(8,128)}, u32[]{:S(2)}) copy-start(f32[96,8,1,1]{1,0,3,2:T(8,128)} %get-tuple-element.655) | copy-start | bytes 9220
  549.2 1.0 copy-start.12
  568.0 1.0 copy-start.13
Sparse Core Ops, SparseCore 0:
  164.1 197.5 all-reduce.50
  364.1 51.9 all-reduce.52
